TPU v7x, 256 devices: a whole 4x4x8 slice. The times are simulated.
256 devices in a mesh: tile: 32 (over z_hi, x, core), grp: 8 (over z_lo, y).
Axes of the slice: x: 4, y: 4, z: 8 (z_hi: 4, z_lo: 2; z = z_hi * 2 + z_lo), core: 2. Of those that a mesh axis runs over, the one named last changes fastest.
Arguments:
- traces: float32 [1024, 16, 1500], P(('tile', 'grp')), may hold values from -6 to 6
- validity: int32 [1024, 16], P(('tile', 'grp')), may hold values 0 or 1
- boundary_rows: int32 [256, 2, 4], P(('tile', 'grp')), may hold values from 0 to 3, as said below
- boundary_count: int32 [256, 2], P(('tile', 'grp')), may hold values from 1 to 4, as said below
- pair_mask: int32 [1024, 96], P(('tile', 'grp')), may hold values from 0 to 1, as said below
Outputs:
- correlations: bfloat16 [1024, 96, 2001], P(('tile', 'grp'))
Inputs may be any that keep to these rules, and one draw needn't show every extreme that they name: `boundary_rows`: each device's list in each direction orders all of its 4 local stations, each once. `boundary_count`: in every draw some device sends all 4 of its stations in each direction. `pair_mask`: a station's column for itself is 0.
All inputs are finite; a program needn't handle non-finite values. No bound on the sum of `validity` on one device may be relied on, other than what follows from the above.
Results may differ from a plain program's by a relative error of at most 0.008.
Values may be sent and summed in bfloat16 or wider, within the bound.
A program may use at most 64 MiB of HBM per device.

v0:
```python
import math
import jax
import jax.numpy as jnp
from jax import lax
from jax.sharding import PartitionSpec as P

SAMP = 1500
NBIN = 144
MAXLAG = 1000
LAGS = 2001


def passed_along(array, axis, by):
    count = lax.axis_size(axis)
    pairs = [(i, i + by) for i in range(count) if 0 <= i + by < count]
    return lax.ppermute(array, axis, pairs)


def fourier_table(samples):
    points = 2 * samples
    sample_number = jnp.arange(samples, dtype=jnp.int32)[:, None]
    freq_number = jnp.arange(1, NBIN + 1, dtype=jnp.int32)[None, :]
    angles = jnp.mod(sample_number * freq_number, points).astype(jnp.float32) * (
        2.0 * jnp.pi / points
    )
    return jnp.concatenate([jnp.cos(angles), -jnp.sin(angles)], axis=1)


def lag_basis():
    points = 2 * SAMP
    freq_number = jnp.arange(1, NBIN + 1, dtype=jnp.int32)[:, None]
    lag_number = jnp.arange(LAGS, dtype=jnp.int32)[None, :] - MAXLAG
    angles = jnp.mod(freq_number * lag_number, points).astype(jnp.float32) * (2.0 * jnp.pi / points)
    return jnp.concatenate([jnp.cos(angles), -jnp.sin(angles)], axis=0)


def whitened(traces, valid_float):
    stations, segments, samples = traces.shape
    sample_number = jnp.arange(samples, dtype=jnp.float32)
    hann_taper = 0.5 - 0.5 * jnp.cos(sample_number * (2.0 * jnp.pi / samples))
    flat_traces = (traces * hann_taper).reshape(stations * segments, samples)
    spectrum = jnp.dot(
        flat_traces,
        fourier_table(samples),
        precision=lax.Precision.HIGHEST,
        preferred_element_type=jnp.float32,
    )
    spectrum = spectrum.reshape(stations, segments, 2, NBIN)
    real_part = spectrum[:, :, 0]
    imag_part = spectrum[:, :, 1]
    power_bins = real_part * real_part + imag_part * imag_part
    padded = jnp.pad(power_bins, ((0, 0), (0, 0), (4, 4)))
    smooth = sum((padded[:, :, offset : offset + NBIN] for offset in range(9))) / 9.0
    mean_power = jnp.mean(power_bins, axis=2, keepdims=True)
    factor = valid_float[:, :, None] / jnp.sqrt(0.5 * smooth + 0.5 * mean_power + 1e-06)
    return jnp.stack([real_part * factor, imag_part * factor], axis=2).astype(jnp.bfloat16)


def stacked(left_spec, left_mask, right_spec, right_mask):
    left_both = jnp.concatenate([left_spec[:, :, 0], left_spec[:, :, 1]], axis=1)
    right_real = right_spec[:, :, 0]
    right_imag = right_spec[:, :, 1]
    right_both = jnp.stack(
        [
            jnp.concatenate([right_real, right_imag], axis=1),
            jnp.concatenate([-right_imag, right_real], axis=1),
        ],
        axis=1,
    )
    product = jnp.einsum(
        "iqf,jcqf->ijcf", left_both, right_both, preferred_element_type=jnp.float32
    )
    pair_count = jnp.einsum("iq,jq->ij", left_mask, right_mask, preferred_element_type=jnp.float32)
    return (product / jnp.maximum(pair_count, 1.0)[:, :, None, None]).astype(jnp.bfloat16)


def on_device(traces, validity, boundary_rows, boundary_count, pair_mask):
    per_device = traces.shape[0]
    valid_float = validity.astype(jnp.float32)
    valid_half = validity.astype(jnp.bfloat16)
    own_spec = whitened(traces, valid_float)
    slot_number = jnp.arange(per_device, dtype=jnp.int32)
    live_up = (slot_number < boundary_count[0, 0]).astype(jnp.float32)
    live_down = (slot_number < boundary_count[0, 1]).astype(jnp.float32)
    picks_up = boundary_rows[0, 0]
    picks_down = boundary_rows[0, 1]
    below_traces, below_mask = passed_along(
        (
            jnp.take(traces, picks_up, axis=0) * live_up[:, None, None],
            jnp.take(valid_float, picks_up, axis=0) * live_up[:, None],
        ),
        "tile",
        1,
    )
    above_traces, above_mask = passed_along(
        (
            jnp.take(traces, picks_down, axis=0) * live_down[:, None, None],
            jnp.take(valid_float, picks_down, axis=0) * live_down[:, None],
        ),
        "tile",
        -1,
    )
    recv_spec = whitened(
        jnp.concatenate([below_traces, above_traces], axis=0),
        jnp.concatenate([below_mask, above_mask], axis=0),
    )
    recv_mask = jnp.concatenate([below_mask, above_mask], axis=0).astype(jnp.bfloat16)
    local_spec = jnp.concatenate([own_spec, recv_spec], axis=0)
    local_mask = jnp.concatenate([valid_half, recv_mask], axis=0)
    all_spec, all_mask = (
        lax.all_gather(local_spec, "grp", axis=0, tiled=True),
        lax.all_gather(local_mask, "grp", axis=0, tiled=True),
    )
    cross_spec = stacked(own_spec, valid_half, all_spec, all_mask)
    columns = cross_spec.shape[1]
    basis = lag_basis()
    basis_high = basis.astype(jnp.bfloat16)
    basis_low = (basis - basis_high.astype(jnp.float32)).astype(jnp.bfloat16)
    flat_cross = cross_spec.reshape(per_device * columns, 2 * NBIN)
    series = jnp.dot(flat_cross, basis_high, preferred_element_type=jnp.float32)
    series = series + jnp.dot(flat_cross, basis_low, preferred_element_type=jnp.float32)
    series = series.reshape(per_device, columns, -1)
    scaled = series * (pair_mask.astype(jnp.float32) / math.sqrt(NBIN))[:, :, None]
    return scaled.astype(jnp.bfloat16)


def solution(mesh):
    return jax.shard_map(
        on_device,
        mesh=mesh,
        in_specs=(
            P(("tile", "grp"), None, None),
            P(("tile", "grp"), None),
            P(("tile", "grp"), None, None),
            P(("tile", "grp"), None),
            P(("tile", "grp"), None),
        ),
        out_specs=P(("tile", "grp"), None, None),
        check_vma=False,
    )
```

profile of v0, /device:TPU:184, one launch (start us, length us, event | category | flops | bytes accessed | tf_op | source)
XLA Modules:
  0.0 117.1 jit_solution(16800844627624242405)
XLA Ops:
  0.0 1.3 %fusion.42 = (s32[1,1]{1,0:T(1,128)}, s32[1,1]{1,0:T(1,128)}) fusion(s32[1,2]{1,0:T(1,128)} %param.12), kind=kLoop, calls=%fused_computation.103 | loop fusion | bytes 16 | tf_op jit(solution)/shard_map/slice | solution.py:83
  1.3 1.4 %compare_and_fusion.1 = (pred[4]{0:T(512)(128)(4,1)S(1)}, s32[4]{0:T(128)S(1)}, pred[4]{0:T(512)(128)(4,1)S(1)}, s32[4]{0:T(128)S(1)}, f32[4]{0:T(128)S(1)}) fusion(s32[1,2,4]{2,1,0:T(2,128)} %param.11, s32[]{:T(128)} %bitcast.12), kind=kLoop, calls=%fused_computation.90 | loop fusion | flops 56 | bytes 92 | tf_op jit(solution)/shard_map/jit(_take)/and | solution.py:89
  2.8 1.6 %gather_fusion.1 = f32[4,16,1500]{2,1,0:T(8,128)S(1)} fusion(f32[4,16,1500]{2,1,0:T(8,128)} %param.9, s32[1024]{0:T(1024)S(1)} %pad_clamp_fusion), kind=kCustom, calls=%fused_computation.2.clone | custom fusion | bytes 768016 | tf_op jit(solution)/shard_map/jit(_take)/gather | solution.py:97
  4.4 4.1 %collective-permute-start.1 = (f32[4,16,1500]{2,1,0:T(8,128)S(1)}, f32[4,16,1500]{2,1,0:T(8,128)S(1)}, u32[]{:S(2)}, u32[]{:S(2)}) collective-permute-start(f32[4,16,1500]{2,1,0:T(8,128)S(1)} %select_multiply_fusion), channel_id=1, source_target_pairs={{8,0},{16,8},{24,16},{32,24},{40,32},{48,40},{56,48},{64,56},{72,6... | collective-permute-start | bytes 1152008 | tf_op jit(solution)/shard_map/ppermute | solution.py:16
  8.6 0.6 gather_fusion
  9.2 0.7 compare_convert_fusion.1
  9.9 1.9 %collective-permute-start = (f32[4,16,1500]{2,1,0:T(8,128)S(1)}, f32[4,16,1500]{2,1,0:T(8,128)}, u32[]{:S(2)}, u32[]{:S(2)}) collective-permute-start(f32[4,16,1500]{2,1,0:T(8,128)S(1)} %select_multiply_fusion.1), channel_id=1, source_target_pairs={{0,8},{8,16},{16,24},{24,32},{32,40},{40,48},{48,56},{56,64},{64,7... | collective-permute-start | bytes 1152008 | tf_op jit(solution)/shard_map/ppermute | solution.py:16
  11.9 0.6 gather_fusion.3
  12.5 7.9 %collective-permute-start.3 = (f32[4,16]{1,0:T(4,128)S(1)}, f32[4,16]{1,0:T(4,128)S(1)}, u32[]{:S(2)}, u32[]{:S(2)}) collective-permute-start(f32[4,16]{1,0:T(4,128)S(1)} %select_multiply_fusion.2), channel_id=1, source_target_pairs={{8,0},{16,8},{24,16},{32,24},{40,32},{48,40},{56,48},{64,56},{72,6... | collective-permute-start | bytes 776 | tf_op jit(solution)/shard_map/ppermute | solution.py:16
  21.0 1.9 %collective-permute-start.2 = (f32[4,16]{1,0:T(4,128)S(1)}, f32[4,16]{1,0:T(4,128)S(1)}, u32[]{:S(2)}, u32[]{:S(2)}) collective-permute-start(f32[4,16]{1,0:T(4,128)S(1)} %select_multiply_fusion.3), channel_id=1, source_target_pairs={{0,8},{8,16},{16,24},{24,32},{32,40},{40,48},{48,56},{56,64},{64,7... | collective-permute-start | bytes 776 | tf_op jit(solution)/shard_map/ppermute | solution.py:16
  23.0 3.7 %fusion.16 = (f32[1500,144]{0,1:T(8,128)S(1)}, f32[1500,144]{0,1:T(8,128)S(1)}) fusion(s32[144]{0:T(256)S(1)} %iota_add_fusion.1), kind=kLoop, calls=%fused_computation.35 | loop fusion | flops 2160000 | bytes 1728576 | tf_op jit(solution)/shard_map/cos | solution.py:26
  26.8 1.9 %fusion.23 = f32[4,16,2,144]{3,1,2,0:T(8,128)S(1)} fusion(f32[2,144,1500,1]{2,1,0,3:T(8,128)S(1)} %bitcast.98, f32[4,16,1500]{2,1,0:T(8,128)S(1)} %copy-done.4, f32[1500]{0:T(1024)S(1)} %multiply_subtract_fusion), kind=kOutput, calls=%fused_computation.44 | convolution fusion | flops 331872000 | bytes 2191728 | tf_op jit(solution)/shard_map/dot_general | solution.py:42
  29.1 6.1 %fusion.9 = (f32[144,2001]{1,0:T(8,128)}, f32[144,2001]{1,0:T(8,128)}) fusion(s32[2001]{0:T(1024)S(1)} %iota_add_fusion, s32[144]{0:T(256)S(1)} %iota_add_fusion.1), kind=kLoop, calls=%fused_computation.25 | loop fusion | flops 2881440 | bytes 2313732 | tf_op jit(solution)/shard_map/cos | solution.py:34
  35.4 28.1 %all-gather = bf16[8,12,16]{2,1,0:T(8,128)(2,1)S(1)} all-gather(bf16[1,12,16]{2,1,0:T(8,128)(2,1)S(1)} %maximum_bitcast_fusion.3), channel_id=1, replica_groups=mesh['tile'=32,'grp'=8] {'grp'}, dimensions={0}, use_global_device_ids=true | all-gather | bytes 3456 | tf_op jit(solution)/shard_map/all_gather | solution.py:112
  63.7 2.7 %fusion.19 = f32[8,16,2,144]{3,1,2,0:T(8,128)S(1)} fusion(f32[2,144,1500,1]{2,1,0,3:T(8,128)S(1)} %bitcast.99, f32[4,16,1500]{2,1,0:T(8,128)S(1)} %collective-permute-done.1, f32[4,16,1500]{2,1,0:T(8,128)} %collective-permute-done, f32[1500]{0:T(1024)S(1)} %multiply_subtract_fusion), kind=kOutput, calls=%fused_computation.41 | convolution fusion | flops 663936000 | bytes 2649456 | tf_op jit(solution)/shard_map/dot_general | solution.py:42
  66.9 31.8 %all_gather.6 = bf16[96,16,2,144]{3,1,0,2:T(8,128)(2,1)S(1)} all-gather(bf16[12,16,2,144]{3,1,0,2:T(8,128)(2,1)S(1)} %maximum_maximum_fusion), channel_id=1, replica_groups=mesh['tile'=32,'grp'=8] {'grp'}, dimensions={0}, use_global_device_ids=true | all-gather | bytes 995328 | tf_op jit(solution)/shard_map/all_gather | solution.py:111
  98.9 0.7 maximum_bitcast_fusion
  99.6 0.6 pad_maximum_fusion
  100.2 5.5 %copy.20 = bf16[96,2,32,144]{0,2,1,3:T(8,128)(2,1)} copy(bf16[96,2,32,144]{3,2,0,1:T(8,128)(2,1)S(1)} %pad_maximum_fusion) | data formatting | bytes 3538944 | tf_op jit(solution)/shard_map/stack | solution.py:63
  105.7 2.3 %fusion.4 = bf16[4,96,2,144]{1,0,2,3:T(4,128)(2,1)S(1)} fusion(bf16[96,2,32,144]{0,2,1,3:T(8,128)(2,1)} %copy.20, bf16[4,32,144,1]{1,0,3,2:T(4,128)(2,1)S(1)} %copy.27, f32[4,96]{1,0:T(4,128)S(1)} %fusion.11), kind=kOutput, calls=%fused_computation.18 | convolution fusion | flops 7299072 | bytes 2029056 | tf_op jit(solution)/shard_map/iqf,jcqf->ijcf/dot_general | solution.py:70
  108.3 1.3 %fusion.1 = f32[384,2001]{0,1:T(8,128)S(1)} fusion(bf16[384,288]{0,1:T(8,128)(2,1)S(1)} %reshape.85, f32[144,2001]{1,0:T(8,128)S(1)} %copy-done.2, f32[144,2001]{1,0:T(8,128)S(1)} %copy-done), kind=kOutput, calls=%fused_computation.14 | convolution fusion | flops 444894336 | bytes 5599872 | tf_op jit(solution)/shard_map/dot_general | solution.py:120
  109.9 1.3 %convolution_add_fusion = f32[384,2001]{0,1:T(8,128)S(1)} fusion(f32[384,2001]{0,1:T(8,128)S(1)} %fusion.1, bf16[384,288]{0,1:T(8,128)(2,1)S(1)} %reshape.85, f32[144,2001]{1,0:T(8,128)S(1)} %copy-done.3, f32[144,2001]{1,0:T(8,128)S(1)} %copy-done.1), kind=kOutput, calls=%fused_computation.6 | convolution fusion | flops 446239008 | bytes 8673408 | tf_op jit(solution)/shard_map/dot_general | solution.py:121
  111.3 2.6 %copy.24 = f32[384,2001]{1,0:T(8,128)} copy(f32[384,2001]{0,1:T(8,128)S(1)} %convolution_add_fusion) | data formatting | bytes 6147072 | tf_op jit(solution)/shard_map/add | solution.py:121
  113.8 3.3 %multiply_convert_fusion = bf16[4,96,2001]{2,1,0:T(8,128)(2,1)} fusion(f32[4,96,2001]{2,1,0:T(8,128)} %bitcast.100, f32[4,96]{1,0:T(4,128)S(1)} %convert_multiply_fusion), kind=kLoop, calls=%fused_computation.5 | loop fusion | flops 1536768 | bytes 4611840 | tf_op jit(solution)/shard_map/convert_element_type | solution.py:124
  (51 shorter events, 3.2 us)
Async XLA Ops:
  0.0 8.6 %copy-start.4 = (f32[4,16,1500]{2,1,0:T(8,128)S(1)}, f32[4,16,1500]{2,1,0:T(8,128)}, u32[]{:S(2)}) copy-start(f32[4,16,1500]{2,1,0:T(8,128)} %param.9) | copy-start | bytes 1152004
  2.7 9.1 %copy-start.5 = (s32[4,16]{1,0:T(4,128)S(1)}, s32[4,16]{1,0:T(4,128)}, u32[]{:S(2)}) copy-start(s32[4,16]{1,0:T(4,128)} %param.10) | copy-start | bytes 772
  4.4 59.2 %collective-permute-start.1 = (f32[4,16,1500]{2,1,0:T(8,128)S(1)}, f32[4,16,1500]{2,1,0:T(8,128)S(1)}, u32[]{:S(2)}, u32[]{:S(2)}) collective-permute-start(f32[4,16,1500]{2,1,0:T(8,128)S(1)} %select_multiply_fusion), channel_id=1, source_target_pairs={{8,0},{16,8},{24,16},{32,24},{40,32},{48,40},{56,48},{64,56},{72,6... | collective-permute-start | bytes 1152008 | tf_op jit(solution)/shard_map/ppermute | solution.py:16
  9.9 53.7 %collective-permute-start = (f32[4,16,1500]{2,1,0:T(8,128)S(1)}, f32[4,16,1500]{2,1,0:T(8,128)}, u32[]{:S(2)}, u32[]{:S(2)}) collective-permute-start(f32[4,16,1500]{2,1,0:T(8,128)S(1)} %select_multiply_fusion.1), channel_id=1, source_target_pairs={{0,8},{8,16},{16,24},{24,32},{32,40},{40,48},{48,56},{56,64},{64,7... | collective-permute-start | bytes 1152008 | tf_op jit(solution)/shard_map/ppermute | solution.py:16
  12.5 22.9 %collective-permute-start.3 = (f32[4,16]{1,0:T(4,128)S(1)}, f32[4,16]{1,0:T(4,128)S(1)}, u32[]{:S(2)}, u32[]{:S(2)}) collective-permute-start(f32[4,16]{1,0:T(4,128)S(1)} %select_multiply_fusion.2), channel_id=1, source_target_pairs={{8,0},{16,8},{24,16},{32,24},{40,32},{48,40},{56,48},{64,56},{72,6... | collective-permute-start | bytes 776 | tf_op jit(solution)/shard_map/ppermute | solution.py:16
  21.0 14.4 %collective-permute-start.2 = (f32[4,16]{1,0:T(4,128)S(1)}, f32[4,16]{1,0:T(4,128)S(1)}, u32[]{:S(2)}, u32[]{:S(2)}) collective-permute-start(f32[4,16]{1,0:T(4,128)S(1)} %select_multiply_fusion.3), channel_id=1, source_target_pairs={{0,8},{8,16},{16,24},{24,32},{32,40},{40,48},{48,56},{56,64},{64,7... | collective-permute-start | bytes 776 | tf_op jit(solution)/shard_map/ppermute | solution.py:16
  28.7 6.5 %copy-start.6 = (s32[4,96]{1,0:T(4,128)S(1)}, s32[4,96]{1,0:T(4,128)}, u32[]{:S(2)}) copy-start(s32[4,96]{1,0:T(4,128)} %param.13) | copy-start | bytes 4612
  105.7 2.6 %copy-start = (f32[144,2001]{1,0:T(8,128)S(1)}, f32[144,2001]{1,0:T(8,128)}, u32[]{:S(2)}) copy-start(f32[144,2001]{1,0:T(8,128)} %get-tuple-element.23) | copy-start | bytes 3457732
  105.7 2.6 %copy-start.2 = (f32[144,2001]{1,0:T(8,128)S(1)}, f32[144,2001]{1,0:T(8,128)}, u32[]{:S(2)}) copy-start(f32[144,2001]{1,0:T(8,128)} %get-tuple-element.24) | copy-start | bytes 3457732
  108.3 1.3 %copy-start.1 = (f32[144,2001]{1,0:T(8,128)S(1)}, f32[144,2001]{1,0:T(8,128)}, u32[]{:S(2)}) copy-start(f32[144,2001]{1,0:T(8,128)} %get-tuple-element.23) | copy-start | bytes 3457732
  108.3 1.6 %copy-start.3 = (f32[144,2001]{1,0:T(8,128)S(1)}, f32[144,2001]{1,0:T(8,128)}, u32[]{:S(2)}) copy-start(f32[144,2001]{1,0:T(8,128)} %get-tuple-element.24) | copy-start | bytes 3457732
where the time goes:
time: 117 us
  blocking collectives  59.9 us (51%)
  other arithmetic  17.9 us (15%)
  starting transfers between devices  15.8 us (14%)
  local copies, waits for them, and re-layouts  13.6 us (12%)
  matrix products  9.57 us (8%)
    all_gather x1, blocking collectives, on_device(): lax.all_gather(local_spec, 'grp', axis=0, tiled=True)  31.8 us
    all_gather x1, blocking collectives, on_device(): lax.all_gather(local_mask, 'grp', axis=0, tiled=True)  28.1 us
    ppermute x4, starting transfers between devices, passed_along(): return lax.ppermute(array, axis, pairs)  15.8 us
    cos x1, other arithmetic, lag_basis(): return jnp.concatenate([jnp.cos(angles), -jnp.sin(angles)], axis=0)  6.09 us
    another operation x1, local copies, waits for them, and re-layouts, stacked(): jnp.stack([jnp.concatenate([right_real, right_imag], axis=1), jnp.concate...  5.52 us
    dot_general x2, matrix products, whitened(): jnp.dot(flat_traces, fourier_table(samples), precision=lax.Precision.HIGH...  4.58 us
    cos x1, other arithmetic, fourier_table(): return jnp.concatenate([jnp.cos(angles), -jnp.sin(angles)], axis=1)  3.66 us
    convert_element_type x1, other arithmetic, on_device(): return scaled.astype(jnp.bfloat16)  3.26 us
  transfers between devices with their start and end apart: 4, of which 0 were waited for; matrix products, arithmetic and copies ran while one was open for 13% of the time, Pallas kernels for 0%

commit v1 on v0

--- a/solution.py
+++ b/solution.py
@@ -108,7 +108,9 @@
     local_spec = jnp.concatenate([own_spec, recv_spec], axis=0)
     local_mask = jnp.concatenate([valid_half, recv_mask], axis=0)
     all_spec, all_mask = (
-        lax.all_gather(local_spec, "grp", axis=0, tiled=True),
+        jnp.concatenate(
+            lax.all_to_all(jnp.stack([local_spec] * lax.axis_size("grp")), "grp", 0, 0), axis=0
+        ),
         lax.all_gather(local_mask, "grp", axis=0, tiled=True),
     )
     cross_spec = stacked(own_spec, valid_half, all_spec, all_mask)

time: 117 us -> 99.8 us (0.85)
  the two profiles are of different devices: /device:TPU:184 before, /device:TPU:70 now
where the time goes in v1:
time: 99.8 us; the launch traced here: 99.3 us
  blocking collectives  36.1 us (36%)
  starting transfers between devices  19.4 us (19%)
  local copies, waits for them, and re-layouts  17.8 us (18%)
  other arithmetic  17 us (17%)
  matrix products  8.6 us (9%)
    all_gather x1, blocking collectives, on_device(): lax.all_gather(local_mask, 'grp', axis=0, tiled=True)  36.1 us
    ppermute x4, starting transfers between devices, passed_along(): return lax.ppermute(array, axis, pairs)  13.4 us
    all_to_all x1, starting transfers between devices, on_device(): lax.all_to_all(jnp.stack([local_spec] * lax.axis_size('grp')), 'grp', 0, 0)  5.95 us
    unnamed x15, local copies, waits for them, and re-layouts  5.6 us
    cos x1, other arithmetic, lag_basis(): return jnp.concatenate([jnp.cos(angles), -jnp.sin(angles)], axis=0)  4.82 us
    cos x1, other arithmetic, fourier_table(): return jnp.concatenate([jnp.cos(angles), -jnp.sin(angles)], axis=1)  3.66 us
    dot_general x2, matrix products, whitened(): jnp.dot(flat_traces, fourier_table(samples), precision=lax.Precision.HIGH...  3.58 us
    convert_element_type x1, other arithmetic, on_device(): return scaled.astype(jnp.bfloat16)  3.26 us
  transfers between devices with their start and end apart: 5, of which 0 were waited for; matrix products, arithmetic and copies ran while one was open for 15% of the time, Pallas kernels for 0%

profile of v1, /device:TPU:70, one launch (start us, length us, event | category | flops | bytes accessed | tf_op | source)
XLA Modules:
  0.0 99.3 jit_solution(11725721447590808527)
XLA Ops:
  0.0 1.3 %fusion.54 = (s32[1,1]{1,0:T(1,128)}, s32[1,1]{1,0:T(1,128)}) fusion(s32[1,2]{1,0:T(1,128)} %param.12), kind=kLoop, calls=%fused_computation.106 | loop fusion | bytes 16 | tf_op jit(solution)/shard_map/slice | solution.py:83
  1.3 1.3 %compare_and_fusion.1 = (pred[4]{0:T(512)(128)(4,1)S(1)}, s32[4]{0:T(128)S(1)}, pred[4]{0:T(512)(128)(4,1)S(1)}, s32[4]{0:T(128)S(1)}, f32[4]{0:T(128)S(1)}) fusion(s32[1,2,4]{2,1,0:T(2,128)} %param.11, s32[]{:T(128)} %bitcast.12), kind=kLoop, calls=%fused_computation.91 | loop fusion | flops 56 | bytes 92 | tf_op jit(solution)/shard_map/jit(_take)/and | solution.py:89
  2.6 1.6 %gather_fusion.1 = f32[4,16,1500]{2,1,0:T(8,128)S(1)} fusion(f32[4,16,1500]{2,1,0:T(8,128)} %param.9, s32[1024]{0:T(1024)S(1)} %pad_clamp_fusion), kind=kCustom, calls=%fused_computation.2.clone | custom fusion | bytes 768016 | tf_op jit(solution)/shard_map/jit(_take)/gather | solution.py:97
  4.3 2.2 %collective-permute-start.1 = (f32[4,16,1500]{2,1,0:T(8,128)S(1)}, f32[4,16,1500]{2,1,0:T(8,128)S(1)}, u32[]{:S(2)}, u32[]{:S(2)}) collective-permute-start(f32[4,16,1500]{2,1,0:T(8,128)S(1)} %select_multiply_fusion), channel_id=1, source_target_pairs={{8,0},{16,8},{24,16},{32,24},{40,32},{48,40},{56,48},{64,56},{72,6... | collective-permute-start | bytes 1152008 | tf_op jit(solution)/shard_map/ppermute | solution.py:16
  7.1 0.7 compare_convert_fusion.1
  7.9 2.2 %collective-permute-start = (f32[4,16,1500]{2,1,0:T(8,128)S(1)}, f32[4,16,1500]{2,1,0:T(8,128)S(1)}, u32[]{:S(2)}, u32[]{:S(2)}) collective-permute-start(f32[4,16,1500]{2,1,0:T(8,128)S(1)} %select_multiply_fusion.1), channel_id=1, source_target_pairs={{0,8},{8,16},{16,24},{24,32},{32,40},{40,48},{48,56},{56,64},{64,7... | collective-permute-start | bytes 1152008 | tf_op jit(solution)/shard_map/ppermute | solution.py:16
  10.7 3.4 %collective-permute-start.3 = (f32[4,16]{1,0:T(4,128)S(1)}, f32[4,16]{1,0:T(4,128)S(1)}, u32[]{:S(2)}, u32[]{:S(2)}) collective-permute-start(f32[4,16]{1,0:T(4,128)S(1)} %select_multiply_fusion.2), channel_id=1, source_target_pairs={{8,0},{16,8},{24,16},{32,24},{40,32},{48,40},{56,48},{64,56},{72,6... | collective-permute-start | bytes 776 | tf_op jit(solution)/shard_map/ppermute | solution.py:16
  14.7 5.7 %collective-permute-start.2 = (f32[4,16]{1,0:T(4,128)S(1)}, f32[4,16]{1,0:T(4,128)S(1)}, u32[]{:S(2)}, u32[]{:S(2)}) collective-permute-start(f32[4,16]{1,0:T(4,128)S(1)} %select_multiply_fusion.3), channel_id=1, source_target_pairs={{0,8},{8,16},{16,24},{24,32},{32,40},{40,48},{48,56},{56,64},{64,7... | collective-permute-start | bytes 776 | tf_op jit(solution)/shard_map/ppermute | solution.py:16
  20.5 3.7 %fusion.21 = (f32[1500,144]{0,1:T(8,128)S(1)}, f32[1500,144]{0,1:T(8,128)S(1)}) fusion(s32[144]{0:T(256)S(1)} %iota_add_fusion.1), kind=kLoop, calls=%fused_computation.36 | loop fusion | flops 2160000 | bytes 1728576 | tf_op jit(solution)/shard_map/cos | solution.py:26
  24.3 1.9 %fusion.34 = f32[4,16,2,144]{3,1,2,0:T(8,128)S(1)} fusion(f32[2,144,1500,1]{2,1,0,3:T(8,128)S(1)} %bitcast.97, f32[4,16,1500]{2,1,0:T(8,128)S(1)} %copy-done.2, f32[1500]{0:T(1024)S(1)} %multiply_subtract_fusion), kind=kOutput, calls=%fused_computation.45 | convolution fusion | flops 331872000 | bytes 2191728 | tf_op jit(solution)/shard_map/dot_general | solution.py:42
  26.6 1.6 %fusion.30 = f32[8,16,2,144]{3,1,2,0:T(8,128)S(1)} fusion(f32[2,144,1500,1]{2,1,0,3:T(8,128)S(1)} %bitcast.98, f32[4,16,1500]{2,1,0:T(8,128)S(1)} %collective-permute-done.1, f32[4,16,1500]{2,1,0:T(8,128)S(1)} %collective-permute-done, f32[1500]{0:T(1024)S(1)} %multiply_subtract_fusion), kind=kOutput, calls=%fused_computation.42 | convolution fusion | flops 663936000 | bytes 2649456 | tf_op jit(solution)/shard_map/dot_general | solution.py:42
  28.9 1.3 %stack.50 = bf16[8,12,16,2,144]{4,2,3,1,0:T(8,128)(2,1)} broadcast(bf16[12,16,2,144]{3,1,2,0:T(8,128)(2,1)S(1)} %copy.24), dimensions={1,2,3,4} | broadcast | bytes 995328 | tf_op jit(solution)/shard_map/stack | solution.py:112
  30.2 6.0 %all-to-all-start = ((bf16[8,12,16,2,144]{4,2,3,1,0:T(8,128)(2,1)}), bf16[8,12,16,2,144]{4,2,3,1,0:T(8,128)(2,1)}, u32[]{:S(2)}, u32[]{:S(2)}) async-start(bf16[8,12,16,2,144]{4,2,3,1,0:T(8,128)(2,1)} %stack.50), calls=%async_computation | async-start | bytes 3145728 | tf_op jit(solution)/shard_map/all_to_all | solution.py:112
  36.2 0.8 copy.34
  37.0 4.8 %fusion.14 = (f32[144,2001]{1,0:T(8,128)S(1)}, f32[144,2001]{1,0:T(8,128)S(1)}) fusion(s32[2001]{0:T(1024)S(1)} %iota_add_fusion, s32[144]{0:T(256)S(1)} %iota_add_fusion.1), kind=kLoop, calls=%fused_computation.26 | loop fusion | flops 2881440 | bytes 2313732 | tf_op jit(solution)/shard_map/cos | solution.py:34
  41.9 36.1 %all-gather = bf16[8,12,16]{2,1,0:T(8,128)(2,1)S(1)} all-gather(bf16[1,12,16]{2,1,0:T(8,128)(2,1)S(1)} %maximum_bitcast_fusion.3), channel_id=1, replica_groups=mesh['tile'=32,'grp'=8] {'grp'}, dimensions={0}, use_global_device_ids=true | all-gather | bytes 3456 | tf_op jit(solution)/shard_map/all_gather | solution.py:114
  78.2 2.7 %fusion.52 = (bf16[96,16,1,144]{3,1,2,0:T(8,128)(2,1)}, bf16[96,16,1,144]{3,1,2,0:T(8,128)(2,1)}) fusion(bf16[96,16,2,144]{3,1,2,0:T(8,128)(2,1)} %bitcast.21), kind=kLoop, calls=%fused_computation.104 | loop fusion | bytes 1769472 | tf_op jit(solution)/shard_map/slice | solution.py:62
  80.8 2.4 %copy.41 = bf16[96,16,1,144]{0,1,3,2:T(8,128)(2,1)S(1)} copy(bf16[96,16,1,144]{3,1,2,0:T(8,128)(2,1)} %get-tuple-element.19) | data formatting | bytes 884736
  83.3 3.2 %copy.40 = bf16[96,16,1,144]{0,1,3,2:T(8,128)(2,1)} copy(bf16[96,16,1,144]{3,1,2,0:T(8,128)(2,1)} %get-tuple-element.20) | data formatting | bytes 884736
  86.5 1.7 %maximum_bitcast_fusion = (bf16[96,1,32,144]{0,2,1,3:T(8,128)(2,1)S(1)}, bf16[96,1,32,144]{0,2,1,3:T(8,128)(2,1)S(1)}) fusion(bf16[96,16,144]{0,1,2:T(8,128)(2,1)S(1)} %bitcast.100, bf16[96,16,144]{0,1,2:T(8,128)(2,1)} %bitcast.101, bf16[96,16,144]{0,1,2:T(8,128)(2,1)S(1)} %bitcast_negate_fusion), kind=kLoop, calls=%fused_computation.20 | loop fusion | flops 3538944 | bytes 3096576 | tf_op jit(solution)/shard_map/stack | solution.py:63
  89.2 1.3 %fusion.5 = f32[384,2001]{0,1:T(8,128)S(1)} fusion(bf16[384,288]{0,1:T(8,128)(2,1)S(1)} %reshape.91, f32[144,2001]{1,0:T(8,128)S(1)} %get-tuple-element.24, f32[144,2001]{1,0:T(8,128)S(1)} %get-tuple-element.23), kind=kOutput, calls=%fused_computation.15 | convolution fusion | flops 444894336 | bytes 5599872 | tf_op jit(solution)/shard_map/dot_general | solution.py:122
  90.5 3.0 %convolution_add_fusion = f32[384,2001]{0,1:T(8,128)S(1)} fusion(f32[384,2001]{0,1:T(8,128)S(1)} %fusion.5, bf16[384,288]{0,1:T(8,128)(2,1)S(1)} %reshape.91, f32[144,2001]{1,0:T(8,128)} %copy-done.1, f32[144,2001]{1,0:T(8,128)} %copy-done), kind=kOutput, calls=%fused_computation.5 | convolution fusion | flops 446239008 | bytes 8673408 | tf_op jit(solution)/shard_map/dot_general | solution.py:123
  93.5 2.5 %copy.31 = f32[384,2001]{1,0:T(8,128)} copy(f32[384,2001]{0,1:T(8,128)S(1)} %convolution_add_fusion) | data formatting | bytes 6147072 | tf_op jit(solution)/shard_map/add | solution.py:123
  96.0 3.3 %multiply_convert_fusion = bf16[4,96,2001]{2,1,0:T(8,128)(2,1)} fusion(f32[4,96,2001]{2,1,0:T(8,128)} %bitcast.99, f32[4,96]{1,0:T(4,128)S(1)} %convert_multiply_fusion), kind=kLoop, calls=%fused_computation.4 | loop fusion | flops 1536768 | bytes 4611840 | tf_op jit(solution)/shard_map/convert_element_type | solution.py:126
  (52 shorter events, 4.4 us)
Async XLA Ops:
  0.0 6.5 %copy-start.2 = (f32[4,16,1500]{2,1,0:T(8,128)S(1)}, f32[4,16,1500]{2,1,0:T(8,128)}, u32[]{:S(2)}) copy-start(f32[4,16,1500]{2,1,0:T(8,128)} %param.9) | copy-start | bytes 1152004
  2.6 7.4 %copy-start.4 = (s32[4,16]{1,0:T(4,128)S(1)}, s32[4,16]{1,0:T(4,128)}, u32[]{:S(2)}) copy-start(s32[4,16]{1,0:T(4,128)} %param.10) | copy-start | bytes 772
  4.3 22.3 %collective-permute-start.1 = (f32[4,16,1500]{2,1,0:T(8,128)S(1)}, f32[4,16,1500]{2,1,0:T(8,128)S(1)}, u32[]{:S(2)}, u32[]{:S(2)}) collective-permute-start(f32[4,16,1500]{2,1,0:T(8,128)S(1)} %select_multiply_fusion), channel_id=1, source_target_pairs={{8,0},{16,8},{24,16},{32,24},{40,32},{48,40},{56,48},{64,56},{72,6... | collective-permute-start | bytes 1152008 | tf_op jit(solution)/shard_map/ppermute | solution.py:16
  7.9 18.8 %collective-permute-start = (f32[4,16,1500]{2,1,0:T(8,128)S(1)}, f32[4,16,1500]{2,1,0:T(8,128)S(1)}, u32[]{:S(2)}, u32[]{:S(2)}) collective-permute-start(f32[4,16,1500]{2,1,0:T(8,128)S(1)} %select_multiply_fusion.1), channel_id=1, source_target_pairs={{0,8},{8,16},{16,24},{24,32},{32,40},{40,48},{48,56},{56,64},{64,7... | collective-permute-start | bytes 1152008 | tf_op jit(solution)/shard_map/ppermute | solution.py:16
  10.7 15.9 %collective-permute-start.3 = (f32[4,16]{1,0:T(4,128)S(1)}, f32[4,16]{1,0:T(4,128)S(1)}, u32[]{:S(2)}, u32[]{:S(2)}) collective-permute-start(f32[4,16]{1,0:T(4,128)S(1)} %select_multiply_fusion.2), channel_id=1, source_target_pairs={{8,0},{16,8},{24,16},{32,24},{40,32},{48,40},{56,48},{64,56},{72,6... | collective-permute-start | bytes 776 | tf_op jit(solution)/shard_map/ppermute | solution.py:16
  14.7 11.9 %collective-permute-start.2 = (f32[4,16]{1,0:T(4,128)S(1)}, f32[4,16]{1,0:T(4,128)S(1)}, u32[]{:S(2)}, u32[]{:S(2)}) collective-permute-start(f32[4,16]{1,0:T(4,128)S(1)} %select_multiply_fusion.3), channel_id=1, source_target_pairs={{0,8},{8,16},{16,24},{24,32},{32,40},{40,48},{48,56},{56,64},{64,7... | collective-permute-start | bytes 776 | tf_op jit(solution)/shard_map/ppermute | solution.py:16
  30.2 6.8 %copy-start.5 = (s32[4,96]{1,0:T(4,128)S(1)}, s32[4,96]{1,0:T(4,128)}, u32[]{:S(2)}) copy-start(s32[4,96]{1,0:T(4,128)} %param.13) | copy-start | bytes 4612
  30.2 47.9 %all-to-all-start = ((bf16[8,12,16,2,144]{4,2,3,1,0:T(8,128)(2,1)}), bf16[8,12,16,2,144]{4,2,3,1,0:T(8,128)(2,1)}, u32[]{:S(2)}, u32[]{:S(2)}) async-start(bf16[8,12,16,2,144]{4,2,3,1,0:T(8,128)(2,1)} %stack.50), calls=%async_computation | async-start | bytes 3145728 | tf_op jit(solution)/shard_map/all_to_all | solution.py:112
  41.9 47.3 %copy-start = (f32[144,2001]{1,0:T(8,128)}, f32[144,2001]{1,0:T(8,128)S(1)}, u32[]{:S(2)}) copy-start(f32[144,2001]{1,0:T(8,128)S(1)} %get-tuple-element.23) | copy-start | bytes 3457732
  41.9 47.3 %copy-start.1 = (f32[144,2001]{1,0:T(8,128)}, f32[144,2001]{1,0:T(8,128)S(1)}, u32[]{:S(2)}) copy-start(f32[144,2001]{1,0:T(8,128)S(1)} %get-tuple-element.24) | copy-start | bytes 3457732
  86.5 1.8 %copy-start.3 = (bf16[4,32,144,1]{1,0,3,2:T(4,128)(2,1)S(1)}, bf16[4,32,144,1]{1,0,3,2:T(4,128)(2,1)}, u32[]{:S(2)}) copy-start(bf16[4,32,144,1]{1,0,3,2:T(4,128)(2,1)} %copy.34) | copy-start | bytes 110596
